TPU v7x, 512 devices: a whole 4x4x16 slice. The times are simulated.
512 devices in a mesh: ctx: 64 (over z, y), head: 8 (over x, core).
Axes of the slice: x: 4, y: 4, z: 16, core: 2. Of those that a mesh axis runs over, the one named last changes fastest.
Arguments:
- query: bfloat16 [65536, 1024], P(('ctx', 'head')), may hold values from -40 to 40
- key_in: bfloat16 [65536, 1024], P(('ctx', 'head')), may hold values from -9 to 9
- value_in: bfloat16 [65536, 1024], P(('ctx', 'head')), may hold values from -6 to 6
- grad_out: bfloat16 [65536, 1024], P(('ctx', 'head')), may hold values from -6 to 6
- random_blocks: int32 [1024, 8, 3], P('ctx', 'head'), may hold values from 0 to 1023, as said below
- universal_segment_indices: int32 [2], replicated, may hold values from 0 to 1023, as said below
Outputs:
- head_results: bfloat16 [65536, 1024], P('ctx', 'head')
- asker_derivative: bfloat16 [65536, 1024], P('ctx', 'head')
- grad_key: bfloat16 [65536, 1024], P('ctx', 'head')
- grad_value: bfloat16 [65536, 1024], P('ctx', 'head')
Inputs may be any that keep to these rules, and one draw needn't show every extreme that they name: `random_blocks`: within one device's share of the lists (16 query blocks, 1 head) at most 2 entries name blocks of one index c of ctx (blocks c * 16 to c * 16 + 15), and in every share some index gets exactly 2. `universal_segment_indices`: the global blocks are different, and one of them is the last block 1023.
All inputs are finite; a program needn't handle non-finite values.
Results may differ from a plain program's by a relative error of at most 0.0075.
Values may be sent and summed in bfloat16 or wider, within the bound.
No kernel may reach another device: no remote copies, remote signals or barrier semaphores. Data moves between devices by JAX's collectives and lax.ppermute only.
A program may use at most 128 MiB of HBM per device.

v0:
```python
import jax
import jax.numpy as jnp
from jax import lax
from jax.sharding import Mesh
from jax.sharding import PartitionSpec as P

FEATURE_LENGTH = 128
SPAN_TOKENS = 64
RANDOM = 3
WORLDWIDE_COUNT = 2
CTX = ("ctx_0", "ctx_1")
CTX_HEAD = ("ctx_0", "ctx_1", "head")


def extended(cells, sides, width):
    for axis, dim in sides:
        count = lax.axis_size(axis)
        ends = count - 1
        head = lax.slice_in_dim(cells, 0, width, axis=dim)
        tail = lax.slice_in_dim(cells, cells.shape[dim] - width, cells.shape[dim], axis=dim)
        cells = jnp.concatenate(
            [
                lax.ppermute(tail, axis, [(i, (i + 1) % count) for i in range(ends)]),
                cells,
                lax.ppermute(head, axis, [((i + 1) % count, i) for i in range(ends)]),
            ],
            axis=dim,
        )
    return cells


def spread(array, axes, root):
    array = jnp.where(lax.axis_index(axes) == root, array, jnp.zeros_like(array))
    for axis in axes:
        array = lax.psum(array, axis)
    return array


def one_axis_at_a_time(array, axes):
    for axis in axes:
        array = lax.pmax(array, axis)
    return array


def over_axes(array, axes):
    for axis in axes:
        array = lax.psum(array, axis)
    return array


def from_behind(array, axis, by):
    devices = lax.axis_size(axis)
    pairs = [(i, i + by) for i in range(devices) if 0 <= i + by < devices]
    return lax.ppermute(array, axis, pairs)


def list_masks(listed, block_total):
    inside = (listed >= 0) & (listed < block_total)
    kept = []
    for slot_pos in range(listed.shape[-1]):
        seen = jnp.zeros(listed.shape[:-1], dtype=jnp.bool_)
        for prior_pos in range(slot_pos):
            seen = seen | inside[..., prior_pos] & (listed[..., prior_pos] == listed[..., slot_pos])
        kept.append(inside[..., slot_pos] & jnp.logical_not(seen))
    return jnp.stack(kept, -1)


def slot_ranks(owners, ctx_count):
    onehot = (owners[..., None] == jnp.arange(ctx_count, dtype=jnp.int32)).astype(jnp.int32)
    before = jnp.cumsum(onehot, axis=-2) - onehot
    return jnp.sum(before * onehot, axis=-1)


def body(query, key_in, value_in, grad_out, random_blocks, universal_segment_indices):
    query, key_in, value_in, grad_out = (
        lax.all_to_all(query, "head", split_axis=1, concat_axis=0, tiled=True),
        lax.all_to_all(key_in, "head", split_axis=1, concat_axis=0, tiled=True),
        lax.all_to_all(value_in, "head", split_axis=1, concat_axis=0, tiled=True),
        lax.all_to_all(grad_out, "head", split_axis=1, concat_axis=0, tiled=True),
    )
    ctx_count = lax.axis_size(CTX)
    ctx_place = lax.axis_index(CTX)
    token_count = query.shape[0]
    head_count = query.shape[1] // FEATURE_LENGTH
    block_count = token_count // SPAN_TOKENS
    block_total = ctx_count * block_count
    request_count = block_count * head_count * RANDOM
    slot_cap = max(2, (5 * request_count + 4 * ctx_count - 1) // (4 * ctx_count))
    inverse_root_dimension = FEATURE_LENGTH ** (-0.5)
    list_width = 3 + RANDOM + WORLDWIDE_COUNT

    def by_head(matrix):
        return matrix.reshape(block_count, SPAN_TOKENS, head_count, FEATURE_LENGTH).transpose(
            0, 2, 1, 3
        )

    def from_head(blocks):
        return blocks.transpose(0, 2, 1, 3).reshape(token_count, head_count * FEATURE_LENGTH)

    query_heads = by_head(query)
    dout_heads = by_head(grad_out)
    paired = jnp.concatenate(
        [
            key_in.reshape(token_count, head_count, FEATURE_LENGTH),
            value_in.reshape(token_count, head_count, FEATURE_LENGTH),
        ],
        2,
    ).reshape(token_count, head_count * 2 * FEATURE_LENGTH)
    padded = extended(paired, ((CTX, 0),), SPAN_TOKENS)
    table_all = padded.reshape(
        block_count + 2, SPAN_TOKENS, head_count, 2 * FEATURE_LENGTH
    ).transpose(0, 2, 1, 3)
    window_sets = jnp.stack(
        [table_all[:block_count], table_all[1 : block_count + 1], table_all[2:]], 2
    )
    local_table = table_all[1 : block_count + 1].reshape(
        block_count * head_count, SPAN_TOKENS, 2 * FEATURE_LENGTH
    )
    head_iota = jnp.arange(head_count, dtype=jnp.int32)[None, :, None]
    owners = (random_blocks // block_count).reshape(-1)
    items = (random_blocks % block_count * head_count + head_iota).reshape(-1)
    slots = owners * slot_cap + slot_ranks(owners, ctx_count)
    requests = (
        jnp.zeros((ctx_count * slot_cap,), jnp.int32)
        .at[slots]
        .set(items)
        .reshape(ctx_count, slot_cap)
    )
    received = lax.all_to_all(requests, CTX, split_axis=0, concat_axis=0, tiled=True)
    fetched = lax.all_to_all(local_table[received], CTX, split_axis=0, concat_axis=0, tiled=True)
    random_sets = fetched.reshape(ctx_count * slot_cap, SPAN_TOKENS, 2 * FEATURE_LENGTH)[
        slots
    ].reshape(block_count, head_count, RANDOM, SPAN_TOKENS, 2 * FEATURE_LENGTH)
    shared_rows = []
    for global_pos in range(WORLDWIDE_COUNT):
        block_id = universal_segment_indices[global_pos]
        start_row = block_id % block_count * SPAN_TOKENS
        piece = jnp.concatenate(
            [
                lax.dynamic_slice_in_dim(matrix, start_row, SPAN_TOKENS, 0)
                for matrix in (query, key_in, value_in, grad_out)
            ],
            1,
        )
        shared_rows.append(spread(piece, CTX, block_id // block_count))
    shared = (
        jnp.stack(shared_rows, 0)
        .reshape(WORLDWIDE_COUNT, SPAN_TOKENS, 4, head_count, FEATURE_LENGTH)
        .transpose(2, 3, 0, 1, 4)
    )
    global_query = shared[0].reshape(head_count, WORLDWIDE_COUNT * SPAN_TOKENS, FEATURE_LENGTH)
    global_dout = shared[3].reshape(head_count, WORLDWIDE_COUNT * SPAN_TOKENS, FEATURE_LENGTH)
    global_pairs = jnp.concatenate([shared[1], shared[2]], -1)
    pair_sets = jnp.concatenate(
        [
            window_sets,
            random_sets,
            jnp.broadcast_to(
                global_pairs[None],
                (block_count, head_count, WORLDWIDE_COUNT, SPAN_TOKENS, 2 * FEATURE_LENGTH),
            ),
        ],
        2,
    )
    collected_lookup_segments = pair_sets[..., :FEATURE_LENGTH]
    collected_content_segments = pair_sets[..., FEATURE_LENGTH:]
    own_ids = ctx_place * block_count + jnp.arange(block_count, dtype=jnp.int32)
    window_ids = jnp.stack([own_ids - 1, own_ids, own_ids + 1], 1)[:, None, :]
    global_cols = jnp.broadcast_to(
        universal_segment_indices[None, None, :], (block_count, head_count, WORLDWIDE_COUNT)
    )
    listed = jnp.concatenate([window_ids, random_blocks, global_cols], 2)
    kept = list_masks(listed, block_total)
    raw_affinities = (
        jnp.einsum(
            "bhqd,bhskd->bhqsk",
            query_heads,
            collected_lookup_segments,
            preferred_element_type=jnp.float32,
        )
        * inverse_root_dimension
    )
    live = kept[:, :, None, :, None]
    row_max = jnp.max(jnp.where(live, raw_affinities, -jnp.inf), axis=(3, 4), keepdims=True)
    normalized_affinities = jnp.where(live, jnp.exp(raw_affinities - row_max), 0.0)
    normalizer_totals = jnp.sum(normalized_affinities, axis=(3, 4))
    sparse_mixture = (
        jnp.einsum(
            "bhqsk,bhskd->bhqd",
            normalized_affinities.astype(jnp.bfloat16),
            collected_content_segments,
            preferred_element_type=jnp.float32,
        )
        / normalizer_totals[..., None]
    ).astype(jnp.bfloat16)
    key_heads = key_in.reshape(token_count, head_count, FEATURE_LENGTH).transpose(1, 0, 2)
    value_heads = value_in.reshape(token_count, head_count, FEATURE_LENGTH).transpose(1, 0, 2)
    global_scores = (
        jnp.einsum("hqd,hkd->hqk", global_query, key_heads, preferred_element_type=jnp.float32)
        * inverse_root_dimension
    )
    global_max = one_axis_at_a_time(jnp.max(global_scores, axis=-1), CTX)
    global_weights = jnp.exp(global_scores - global_max[..., None])
    partial_acc = jnp.einsum(
        "hqk,hkd->hqd",
        global_weights.astype(jnp.bfloat16),
        value_heads,
        preferred_element_type=jnp.float32,
    )
    global_acc, global_total = (
        over_axes(partial_acc, CTX),
        over_axes(jnp.sum(global_weights, axis=-1), CTX),
    )
    universal_mixture = (global_acc / global_total[..., None]).astype(jnp.bfloat16)
    global_blocks = universal_mixture.reshape(
        head_count, WORLDWIDE_COUNT, SPAN_TOKENS, FEATURE_LENGTH
    )
    hits = [
        own_ids == universal_segment_indices[global_pos] for global_pos in range(WORLDWIDE_COUNT)
    ]
    mixed_segments = sparse_mixture
    for global_pos in range(WORLDWIDE_COUNT):
        mixed_segments = jnp.where(
            hits[global_pos][:, None, None, None],
            global_blocks[None, :, global_pos],
            mixed_segments,
        )
    is_global = jnp.any(own_ids[:, None] == universal_segment_indices[None, :], axis=1)
    filtered_upstream = jnp.where(
        is_global[:, None, None, None], jnp.zeros((), jnp.bfloat16), dout_heads
    )
    rowwise_correction = jnp.sum(
        filtered_upstream.astype(jnp.float32) * sparse_mixture.astype(jnp.float32), axis=-1
    )
    probabilities = normalized_affinities / normalizer_totals[..., None, None]
    prob_half = probabilities.astype(jnp.bfloat16)
    affinity_derivative = jnp.einsum(
        "bhqd,bhskd->bhqsk",
        filtered_upstream,
        collected_content_segments,
        preferred_element_type=jnp.float32,
    )
    raw_affinity_derivative = (
        probabilities * (affinity_derivative - rowwise_correction[..., None, None])
    ).astype(jnp.bfloat16)
    grad_q = (
        jnp.einsum(
            "bhqsk,bhskd->bhqd",
            raw_affinity_derivative,
            collected_lookup_segments,
            preferred_element_type=jnp.float32,
        )
        * inverse_root_dimension
    )
    pair_grads = []
    for slot_pos in range(list_width):
        key_part = (
            jnp.einsum(
                "bhqk,bhqd->bhkd",
                raw_affinity_derivative[:, :, :, slot_pos],
                query_heads,
                preferred_element_type=jnp.float32,
            )
            * inverse_root_dimension
        )
        value_part = jnp.einsum(
            "bhqk,bhqd->bhkd",
            prob_half[:, :, :, slot_pos],
            filtered_upstream,
            preferred_element_type=jnp.float32,
        )
        pair_grads.append(jnp.concatenate([key_part, value_part], -1))
    grad_pairs = pair_grads[1]
    grad_pairs = grad_pairs.at[:-1].add(pair_grads[0][1:])
    grad_pairs = grad_pairs.at[1:].add(pair_grads[2][:-1])
    from_next = from_behind(pair_grads[0][0].astype(jnp.bfloat16), CTX, -1).astype(jnp.float32)
    from_prev = from_behind(pair_grads[2][-1].astype(jnp.bfloat16), CTX, 1).astype(jnp.float32)
    grad_pairs = grad_pairs.at[-1].add(from_next).at[0].add(from_prev)
    random_terms = (
        jnp.stack(pair_grads[3 : 3 + RANDOM], 2)
        .astype(jnp.bfloat16)
        .reshape(request_count, SPAN_TOKENS, 2 * FEATURE_LENGTH)
    )
    outgoing = (
        jnp.zeros((ctx_count * slot_cap, SPAN_TOKENS, 2 * FEATURE_LENGTH), jnp.bfloat16)
        .at[slots]
        .set(random_terms)
    )
    returned = lax.all_to_all(
        outgoing.reshape(ctx_count, slot_cap, SPAN_TOKENS, 2 * FEATURE_LENGTH),
        CTX,
        split_axis=0,
        concat_axis=0,
        tiled=True,
    )
    table_grads = (
        jnp.zeros((block_count * head_count, SPAN_TOKENS, 2 * FEATURE_LENGTH), jnp.float32)
        .at[received.reshape(-1)]
        .add(
            returned.reshape(ctx_count * slot_cap, SPAN_TOKENS, 2 * FEATURE_LENGTH).astype(
                jnp.float32
            )
        )
    )
    grad_pairs = grad_pairs + table_grads.reshape(
        block_count, head_count, SPAN_TOKENS, 2 * FEATURE_LENGTH
    )
    global_terms = jnp.stack(
        [
            jnp.sum(pair_grads[3 + RANDOM + global_pos], axis=0)
            for global_pos in range(WORLDWIDE_COUNT)
        ],
        0,
    )
    global_delta = jnp.sum(
        global_dout.astype(jnp.float32) * universal_mixture.astype(jnp.float32), axis=-1
    )
    global_prob = global_weights / global_total[..., None]
    value_local = jnp.einsum(
        "hqk,hqd->hkd",
        global_prob.astype(jnp.bfloat16),
        global_dout,
        preferred_element_type=jnp.float32,
    )
    global_dprob = jnp.einsum(
        "hqd,hkd->hqk", global_dout, value_heads, preferred_element_type=jnp.float32
    )
    global_dscore = (global_prob * (global_dprob - global_delta[..., None])).astype(jnp.bfloat16)
    key_local = (
        jnp.einsum("hqk,hqd->hkd", global_dscore, global_query, preferred_element_type=jnp.float32)
        * inverse_root_dimension
    )
    query_partial = (
        jnp.einsum("hqk,hkd->hqd", global_dscore, key_heads, preferred_element_type=jnp.float32)
        * inverse_root_dimension
    )
    global_terms, universal_asker_derivative = (
        over_axes(global_terms, CTX),
        over_axes(query_partial, CTX),
    )
    local_pairs = jnp.concatenate([key_local, value_local], -1).reshape(
        head_count, block_count, SPAN_TOKENS, 2 * FEATURE_LENGTH
    )
    grad_pairs = grad_pairs + local_pairs.transpose(1, 0, 2, 3)
    global_dq_blocks = universal_asker_derivative.reshape(
        head_count, WORLDWIDE_COUNT, SPAN_TOKENS, FEATURE_LENGTH
    )
    for global_pos in range(WORLDWIDE_COUNT):
        hit_mask = hits[global_pos][:, None, None, None]
        grad_pairs = grad_pairs + jnp.where(hit_mask, global_terms[global_pos][None], 0.0)
        grad_q = jnp.where(hit_mask, global_dq_blocks[None, :, global_pos], grad_q)
    return (
        from_head(mixed_segments),
        from_head(grad_q).astype(jnp.bfloat16),
        from_head(grad_pairs[..., :FEATURE_LENGTH]).astype(jnp.bfloat16),
        from_head(grad_pairs[..., FEATURE_LENGTH:]).astype(jnp.bfloat16),
    )


def solution(mesh):
    torus = Mesh(mesh.devices.reshape(16, 4, mesh.shape["head"]), ("ctx_0", "ctx_1", "head"))
    placed = (
        P(CTX_HEAD, None),
        P(CTX_HEAD, None),
        P(CTX_HEAD, None),
        P(CTX_HEAD, None),
        P(CTX, "head", None),
        P(),
    )
    return jax.shard_map(
        body,
        mesh=torus,
        in_specs=placed,
        out_specs=(P(CTX, "head"), P(CTX, "head"), P(CTX, "head"), P(CTX, "head")),
        check_vma=False,
    )
```

profile of v0, /device:TPU:2, one launch (start us, length us, event | category | flops | bytes accessed | tf_op | source)
XLA Modules:
  0.0 883.1 jit_solution(4818153470860434396)
XLA Ops:
  11.0 18.7 %all-to-all-start.4 = ((s32[64,1,2]{2,1,0:T(1,128)}), s32[64,1,2]{2,1,0:T(1,128)S(1)}, u32[]{:S(2)}, u32[]{:S(2)}) async-start(s32[64,1,2]{2,1,0:T(1,128)} %bitcast.39), calls=%async_computation.4 | async-start | bytes 65536 | tf_op jit(solution)/shard_map/all_to_all | solution.py:129
  30.5 13.8 %all-to-all-done.4 = s32[64,1,2]{2,1,0:T(1,128)S(1)} async-done(((s32[64,1,2]{2,1,0:T(1,128)}), s32[64,1,2]{2,1,0:T(1,128)S(1)}, u32[]{:S(2)}, u32[]{:S(2)}) %all-to-all-start.4) | async-done | bytes 544 | tf_op jit(solution)/shard_map/all_to_all | solution.py:129
  44.3 4.8 all-to-all-start.3
  49.1 1.7 copy_bitcast_fusion.1
  50.8 4.3 all-to-all-done.3
  55.2 4.8 all-to-all-start.2
  59.9 1.7 copy_bitcast_fusion.2
  61.6 4.4 all-to-all-done.2
  66.0 4.8 all-to-all-start.1
  70.8 1.7 copy_bitcast_fusion.3
  72.8 4.1 all-to-all-done.1
  76.9 4.8 all-to-all-start
  81.7 2.8 gather_fusion
  84.5 3.2 all-to-all-done
  87.7 5.8 all-to-all-start.5
  102.5 1.3 broadcast_compare_fusion
  103.9 1.3 collective-permute-start.1
  105.2 4.5 collective-permute-start
  112.3 155.7 %all-reduce.18.cloned.1.call-done = (bf16[64,512]{1,0:T(8,128)(2,1)}, bf16[64,512]{1,0:T(8,128)(2,1)}) async-done(((bf16[64,512]{1,0:T(8,128)(2,1)}, bf16[64,512]{1,0:T(8,128)(2,1)}), (bf16[64,512]{1,0:T(8,128)(2,1)}, bf16[64,512]{1,0:T(8,128)(2,1)})) %all-reduce.18.cloned.1.call-update) | async-done | bytes 131088 | tf_op jit(solution)/shard_map/psum | solution.py:35
  268.0 1.5 stack.54
  269.5 1.5 stack.53
  272.9 64.6 %all-reduce.20.cloned.1.call-done = (bf16[1,64,4,1,128]{4,2,1,3,0:T(4,128)(2,1)}, bf16[1,64,4,1,128]{4,2,1,3,0:T(4,128)(2,1)}) async-done(((bf16[1,64,4,1,128]{4,2,1,3,0:T(4,128)(2,1)}, bf16[1,64,4,1,128]{4,2,1,3,0:T(4,128)(2,1)}), (bf16[1,64,4,1,128]{4,2,1,3,0:T(4,128)(2,1)}, bf16[1,64,4,1,128]{4,2,1,3,0:T(4,128)(2,1)})) %all-reduce.20.cloned.1.call-update) | async-done | bytes 131088 | tf_op jit(solution)/shard_map/psum | solution.py:35
  339.0 31.3 %pmax.14 = f32[1,128]{1,0:T(1,128)S(1)} all-reduce(f32[1,128]{1,0:T(1,128)S(1)} %bitcast.401), channel_id=1, replica_groups=mesh['ctx_0'=16,'ctx_1'=4,'head'=8] {'ctx_0'}, use_global_device_ids=true, to_apply=%region_5.6 | all-reduce | flops 128 | bytes 1024 | tf_op jit(solution)/shard_map/pmax | solution.py:41
  370.3 9.3 %pmax.15 = f32[128]{0:T(128)S(1)} all-reduce(f32[128]{0:T(128)S(1)} %bitcast.404), channel_id=1, replica_groups=mesh['ctx_0'=16,'ctx_1'=4,'head'=8] {'ctx_1'}, use_global_device_ids=true, to_apply=%region_6.7 | all-reduce | flops 128 | bytes 1024 | tf_op jit(solution)/shard_map/pmax | solution.py:41
  380.8 28.4 %psum.90 = f32[1,128]{1,0:T(1,128)S(1)} all-reduce(f32[1,128]{1,0:T(1,128)S(1)} %bitcast.400), channel_id=1, replica_groups=mesh['ctx_0'=16,'ctx_1'=4,'head'=8] {'ctx_0'}, use_global_device_ids=true, to_apply=%region_10.11 | all-reduce | flops 128 | bytes 1024 | tf_op jit(solution)/shard_map/psum | solution.py:47
  409.2 8.4 psum.91
  417.6 94.4 %all-reduce.10.cloned.1.call-done = f32[1,128,128]{2,1,0:T(8,128)} async-done(((f32[1,128,128]{2,1,0:T(8,128)}), f32[1,128,128]{2,1,0:T(8,128)}) %all-reduce.10.cloned.1.call-update) | async-done | bytes 65552 | tf_op jit(solution)/shard_map/psum | solution.py:47
  512.0 54.6 %all-reduce.12.cloned.1.call-done = f32[1,128,128]{2,1,0:T(8,128)} async-done(((f32[1,128,128]{2,1,0:T(8,128)}), f32[1,128,128]{2,1,0:T(8,128)}) %all-reduce.12.cloned.1.call-update) | async-done | bytes 65552 | tf_op jit(solution)/shard_map/psum | solution.py:47
  566.6 1.0 multiply_reduce_fusion.1
  567.7 2.8 gather_fusion.1
  570.5 1.3 constant_dynamic-update-slice_fusion
  571.8 1.2 broadcast_dynamic-update-slice_fusion
  572.9 2.4 select_reduce_fusion
  575.3 1.2 bitcast_reduce_fusion
  576.5 1.1 convert_bitcast_fusion
  579.0 2.4 select_select_fusion
  581.8 1.7 multiply_convert_fusion
  585.0 2.5 broadcast_in_dim.195
  587.5 6.7 scatter_fusion
  594.1 15.1 %all-to-all-start.6 = ((bf16[64,2,64,256]{3,2,1,0:T(8,128)(2,1)}), bf16[64,2,64,256]{3,2,1,0:T(8,128)(2,1)}, u32[]{:S(2)}, u32[]{:S(2)}) async-start(bf16[64,2,64,256]{3,2,1,0:T(8,128)(2,1)} %bitcast.335), calls=%async_computation.6 | async-start | bytes 8388608 | tf_op jit(solution)/shard_map/all_to_all | solution.py:289
  613.6 1.3 collective-permute-start.2
  615.4 4.5 collective-permute-start.3
  623.0 161.2 %all-reduce.16.cloned.1.call-done = (f32[1,128,128]{2,1,0:T(8,128)}, f32[2,1,64,256]{3,2,1,0:T(8,128)}) async-done(((f32[1,128,128]{2,1,0:T(8,128)}, f32[2,1,64,256]{3,2,1,0:T(8,128)}), (f32[1,128,128]{2,1,0:T(8,128)}, f32[2,1,64,256]{3,2,1,0:T(8,128)})) %all-reduce.16.cloned.1.call-update) | async-done | bytes 196624 | tf_op jit(solution)/shard_map/psum | solution.py:47
  784.2 25.9 %psum.93 = bf16[1,2,64,128]{3,2,1,0:T(8,128)(2,1)S(1)} all-reduce(f32[1,2,64,128]{3,2,1,0:T(8,128)} %bitcast.398), channel_id=1, replica_groups=mesh['ctx_0'=16,'ctx_1'=4,'head'=8] {'ctx_1'}, use_global_device_ids=true, to_apply=%region_19.20 | all-reduce | flops 16384 | bytes 98304 | tf_op jit(solution)/shard_map/psum | solution.py:47
  810.1 3.8 fusion.18
  813.9 36.5 %all-reduce.14.cloned.1.call-done = f32[2,1,64,256]{3,2,1,0:T(8,128)} async-done(((f32[2,1,64,256]{3,2,1,0:T(8,128)}), f32[2,1,64,256]{3,2,1,0:T(8,128)}) %all-reduce.14.cloned.1.call-update) | async-done | bytes 131088 | tf_op jit(solution)/shard_map/psum | solution.py:47
  851.3 6.5 bitcast_convert_fusion
  857.9 17.0 %scatter_fusion.1 = f32[16,64,256]{2,1,0:T(8,128)S(1)} fusion(f32[16,64,256]{2,1,0:T(8,128)S(1)} %broadcast_in_dim.194, s32[128]{0:T(128)S(1)} %fusion.60, f32[128,64,256]{2,1,0:T(8,128)} %bitcast_convert_fusion), kind=kCustom, calls=%fused_computation.4 | custom fusion | flops 2097152 | bytes 25166336 | tf_op jit(solution)/shard_map/scatter-add | solution.py:299
  (144 shorter events, 27.7 us)
Async XLA Ops:
  7.2 22.6 %copy-start = (bf16[128,1024]{1,0:T(8,128)(2,1)S(1)}, bf16[128,1024]{1,0:T(8,128)(2,1)}, u32[]{:S(2)}) copy-start(bf16[128,1024]{1,0:T(8,128)(2,1)} %param.17) | copy-start | bytes 786436
  11.0 33.3 %all-to-all-start.4 = ((s32[64,1,2]{2,1,0:T(1,128)}), s32[64,1,2]{2,1,0:T(1,128)S(1)}, u32[]{:S(2)}, u32[]{:S(2)}) async-start(s32[64,1,2]{2,1,0:T(1,128)} %bitcast.39), calls=%async_computation.4 | async-start | bytes 65536 | tf_op jit(solution)/shard_map/all_to_all | solution.py:129
  44.3 10.9 %all-to-all-start.3 = ((bf16[128,8,128]{2,0,1:T(8,128)(2,1)}), bf16[128,8,128]{2,0,1:T(8,128)(2,1)S(1)}, u32[]{:S(2)}, u32[]{:S(2)}) async-start(bf16[128,8,128]{2,0,1:T(8,128)(2,1)} %copy_bitcast_fusion), calls=%async_computation.3 | async-start | bytes 524288 | tf_op jit(solution)/shard_map/all_to_all | solution.py:79
  55.2 10.9 %all-to-all-start.2 = ((bf16[128,8,128]{2,0,1:T(8,128)(2,1)}), bf16[128,8,128]{2,0,1:T(8,128)(2,1)S(1)}, u32[]{:S(2)}, u32[]{:S(2)}) async-start(bf16[128,8,128]{2,0,1:T(8,128)(2,1)} %copy_bitcast_fusion.1), calls=%async_computation.2 | async-start | bytes 524288 | tf_op jit(solution)/shard_map/all_to_all | solution.py:78
  66.0 10.9 %all-to-all-start.1 = ((bf16[128,8,128]{2,0,1:T(8,128)(2,1)}), bf16[128,8,128]{2,0,1:T(8,128)(2,1)S(1)}, u32[]{:S(2)}, u32[]{:S(2)}) async-start(bf16[128,8,128]{2,0,1:T(8,128)(2,1)} %copy_bitcast_fusion.2), calls=%async_computation.1 | async-start | bytes 524288 | tf_op jit(solution)/shard_map/all_to_all | solution.py:77
  76.9 10.9 %all-to-all-start = ((bf16[128,8,128]{2,0,1:T(8,128)(2,1)}), bf16[128,8,128]{2,0,1:T(8,128)(2,1)S(1)}, u32[]{:S(2)}, u32[]{:S(2)}) async-start(bf16[128,8,128]{2,0,1:T(8,128)(2,1)} %copy_bitcast_fusion.3), calls=%async_computation | async-start | bytes 524288 | tf_op jit(solution)/shard_map/all_to_all | solution.py:76
  87.7 5.9 copy-start.8
  87.7 11.7 %copy-start.7 = (s32[16,1,3]{0,1,2:T(1,128)S(1)}, s32[16,1,3]{0,1,2:T(1,128)}, u32[]{:S(2)}) copy-start(s32[16,1,3]{0,1,2:T(1,128)} %param.18) | copy-start | bytes 580
  87.7 479.9 %all-to-all-start.5 = ((bf16[64,2,64,256]{3,2,1,0:T(8,128)(2,1)}), bf16[64,2,64,256]{3,2,1,0:T(8,128)(2,1)}, u32[]{:S(2)}, u32[]{:S(2)}) async-start(bf16[64,2,64,256]{3,2,1,0:T(8,128)(2,1)} %bitcast.346), calls=%async_computation.5 | async-start | bytes 8388608 | tf_op jit(solution)/shard_map/all_to_all | solution.py:130
  93.5 174.5 %all-reduce.18.cloned.1.call-start = ((), (), s32[]{:S(2)}) async-start(), calls=%async_computation.11 | async-start | bytes 262144 | tf_op jit(solution)/shard_map/psum | solution.py:35
  103.9 6.8 collective-permute-start.1
  105.2 6.1 collective-permute-start
  110.6 226.9 %all-reduce.20.cloned.1.call-start = ((), (), s32[]{:S(2)}) async-start(), calls=%async_computation.12 | async-start | bytes 262144 | tf_op jit(solution)/shard_map/psum | solution.py:35
  271.0 241.0 %all-reduce.10.cloned.1.call-start = ((), (), s32[]{:S(2)}) async-start(), calls=%async_computation.7 | async-start | bytes 131072 | tf_op jit(solution)/shard_map/psum | solution.py:47
  380.5 186.1 %all-reduce.12.cloned.1.call-start = ((), (), s32[]{:S(2)}) async-start(), calls=%async_computation.8 | async-start | bytes 131072 | tf_op jit(solution)/shard_map/psum | solution.py:47
  576.4 2.6 copy-start.6
  577.5 6.4 copy-start.2
  583.4 1.4 copy-start.4
  594.1 257.1 %all-to-all-start.6 = ((bf16[64,2,64,256]{3,2,1,0:T(8,128)(2,1)}), bf16[64,2,64,256]{3,2,1,0:T(8,128)(2,1)}, u32[]{:S(2)}, u32[]{:S(2)}) async-start(bf16[64,2,64,256]{3,2,1,0:T(8,128)(2,1)} %bitcast.335), calls=%async_computation.6 | async-start | bytes 8388608 | tf_op jit(solution)/shard_map/all_to_all | solution.py:289
  609.2 174.9 %all-reduce.16.cloned.1.call-start = ((), (), s32[]{:S(2)}) async-start(), calls=%async_computation.10 | async-start | bytes 393216 | tf_op jit(solution)/shard_map/psum | solution.py:47
  611.1 1.6 copy-start.5
  611.1 2.2 copy-start.3
  613.6 9.3 %collective-permute-start.2 = (bf16[1,64,256]{2,1,0:T(8,128)(2,1)S(1)}, bf16[1,64,256]{2,1,0:T(8,128)(2,1)S(1)}, u32[]{:S(2)}, u32[]{:S(2)}) collective-permute-start(bf16[1,64,256]{2,1,0:T(8,128)(2,1)S(1)} %fusion.54), channel_id=1, source_target_pairs={{8,0},{16,8},{24,16},{32,24},{40,32},{48,40},{56,48},{64,56},{72,6... | collective-permute-start | bytes 98312 | tf_op jit(solution)/shard_map/ppermute | solution.py:54
  615.4 7.5 collective-permute-start.3
  622.9 227.5 %all-reduce.14.cloned.1.call-start = ((), (), s32[]{:S(2)}) async-start(), calls=%async_computation.9 | async-start | bytes 262144 | tf_op jit(solution)/shard_map/psum | solution.py:47
  857.9 18.3 %copy-start.1 = (bf16[128,1024]{1,0:T(8,128)(2,1)S(1)}, bf16[128,1024]{1,0:T(8,128)(2,1)}, u32[]{:S(2)}) copy-start(bf16[128,1024]{1,0:T(8,128)(2,1)} %param.17) | copy-start | bytes 786436
Sparse Core Ops, SparseCore 0:
  110.7 157.2 all-reduce.17
  271.2 66.2 all-reduce.19
  380.6 131.3 all-reduce.9
  514.2 52.4 all-reduce.11
  623.0 161.1 all-reduce.15
  786.3 64.0 all-reduce.13
where the time goes:
time: 885 us; the launch traced here: 883 us
  waiting for transfers between devices  598 us (68%)
  blocking collectives  103 us (12%)
  starting transfers between devices  70.7 us (8%)
  other arithmetic  37.8 us (4%)
  local copies, waits for them, and re-layouts  35.4 us (4%)
  between operations  21.4 us (2%)
  matrix products  17 us (2%)
    psum x4, waiting for transfers between devices, over_axes(): array = lax.psum(array, axis)  347 us
    psum x2, waiting for transfers between devices, spread(): array = lax.psum(array, axis)  220 us
    psum x3, blocking collectives, over_axes(): array = lax.psum(array, axis)  62.7 us
    pmax x2, blocking collectives, one_axis_at_a_time(): array = lax.pmax(array, axis)  40.5 us
    all_to_all x1, starting transfers between devices, body(): lax.all_to_all(requests, CTX, split_axis=0, concat_axis=0, tiled=True)  18.7 us
  transfers between devices with their start and end apart: 17, of which 12 were waited for; matrix products, arithmetic and copies ran while one was open for 4% of the time, Pallas kernels for 0%

commit v1 on v0

--- a/solution.py
+++ b/solution.py
@@ -44,7 +44,8 @@
 
 def over_axes(array, axes):
     for axis in axes:
-        array = lax.psum(array, axis)
+        pieces = lax.all_gather(array, axis, axis=0, tiled=False)
+        array = pieces.sum(axis=0)
     return array
 
 

time: 885 us -> 737 us (0.83)
  the two profiles are of different devices: /device:TPU:2 before, /device:TPU:66 now
where the time goes in v1:
time: 737 us; the launch traced here: 735 us
  waiting for transfers between devices  424 us (58%)
  blocking collectives  114 us (15%)
  starting transfers between devices  71.2 us (10%)
  other arithmetic  41.9 us (6%)
  local copies, waits for them, and re-layouts  37.5 us (5%)
  matrix products  25.1 us (3%)
  between operations  21.1 us (3%)
    psum x2, waiting for transfers between devices, spread(): array = lax.psum(array, axis)  209 us
    all_gather x3, waiting for transfers between devices, over_axes(): pieces = lax.all_gather(array, axis, axis=0, tiled=False)  131 us
    all_gather x5, blocking collectives, over_axes(): pieces = lax.all_gather(array, axis, axis=0, tiled=False)  75.3 us
    ppermute x2, waiting for transfers between devices, from_behind(): return lax.ppermute(array, axis, pairs)  51.5 us
    pmax x2, blocking collectives, one_axis_at_a_time(): array = lax.pmax(array, axis)  38.2 us
    all_to_all x1, starting transfers between devices, body(): lax.all_to_all(requests, CTX, split_axis=0, concat_axis=0, tiled=True)  17.9 us
    scatter-add x1, other arithmetic, body(): table_grads = jnp.zeros((block_count * head_count, SPAN_TOKENS, 2 * FEATU...  17 us
  transfers between devices with their start and end apart: 16, of which 13 were waited for; matrix products, arithmetic and copies ran while one was open for 6% of the time, Pallas kernels for 0%

profile of v1, /device:TPU:66, one launch (start us, length us, event | category | flops | bytes accessed | tf_op | source)
XLA Modules:
  0.0 734.7 jit_solution(8878274706948725324)
XLA Ops:
  11.0 17.9 %all-to-all-start.4 = ((s32[64,1,2]{2,1,0:T(1,128)}), s32[64,1,2]{2,1,0:T(1,128)S(1)}, u32[]{:S(2)}, u32[]{:S(2)}) async-start(s32[64,1,2]{2,1,0:T(1,128)} %bitcast.41), calls=%async_computation.4 | async-start | bytes 65536 | tf_op jit(solution)/shard_map/all_to_all | solution.py:130
  29.7 11.8 %all-to-all-done.4 = s32[64,1,2]{2,1,0:T(1,128)S(1)} async-done(((s32[64,1,2]{2,1,0:T(1,128)}), s32[64,1,2]{2,1,0:T(1,128)S(1)}, u32[]{:S(2)}, u32[]{:S(2)}) %all-to-all-start.4) | async-done | bytes 544 | tf_op jit(solution)/shard_map/all_to_all | solution.py:130
  41.5 4.8 all-to-all-start
  46.3 1.7 copy_bitcast_fusion.2
  48.0 4.3 all-to-all-done
  52.3 4.8 all-to-all-start.1
  57.1 1.7 copy_bitcast_fusion.1
  58.8 4.4 all-to-all-done.1
  63.2 4.8 all-to-all-start.2
  68.0 1.7 copy_bitcast_fusion
  70.0 4.1 all-to-all-done.2
  74.1 4.8 all-to-all-start.3
  78.9 2.8 gather_fusion
  81.7 3.2 all-to-all-done.3
  84.9 7.7 %all-to-all-start.5 = ((bf16[64,2,64,256]{3,2,1,0:T(8,128)(2,1)}), bf16[64,2,64,256]{3,2,1,0:T(8,128)(2,1)}, u32[]{:S(2)}, u32[]{:S(2)}) async-start(bf16[64,2,64,256]{3,2,1,0:T(8,128)(2,1)} %bitcast.351), calls=%async_computation.5 | async-start | bytes 8388608 | tf_op jit(solution)/shard_map/all_to_all | solution.py:131
  99.6 154.3 %all-reduce.5.cloned.1.call-done = (bf16[64,512]{1,0:T(8,128)(2,1)}, bf16[64,512]{1,0:T(8,128)(2,1)}) async-done(((bf16[64,512]{1,0:T(8,128)(2,1)}, bf16[64,512]{1,0:T(8,128)(2,1)}), (bf16[64,512]{1,0:T(8,128)(2,1)}, bf16[64,512]{1,0:T(8,128)(2,1)})) %all-reduce.5.cloned.1.call-update) | async-done | bytes 131088 | tf_op jit(solution)/shard_map/psum | solution.py:35
  257.7 54.8 %all-reduce.7.cloned.1.call-done = (bf16[1,64,4,1,128]{4,1,0,3,2:T(8,128)(2,1)}, bf16[1,64,4,1,128]{4,1,0,3,2:T(8,128)(2,1)}) async-done(((bf16[1,64,4,1,128]{4,1,0,3,2:T(8,128)(2,1)}, bf16[1,64,4,1,128]{4,1,0,3,2:T(8,128)(2,1)}), (bf16[1,64,4,1,128]{4,1,0,3,2:T(8,128)(2,1)}, bf16[1,64,4,1,128]{4,1,0,3,2:T(8,128)(2,1)})) %all-reduce.7.cloned.1.call-update) | async-done | bytes 131088 | tf_op jit(solution)/shard_map/psum | solution.py:35
  313.7 29.0 %pmax.14 = f32[1,128]{1,0:T(1,128)S(1)} all-reduce(f32[1,128]{1,0:T(1,128)S(1)} %bitcast.411), channel_id=1, replica_groups=mesh['ctx_0'=16,'ctx_1'=4,'head'=8] {'ctx_0'}, use_global_device_ids=true, to_apply=%region_5.6 | all-reduce | flops 128 | bytes 1024 | tf_op jit(solution)/shard_map/pmax | solution.py:41
  342.7 9.3 %pmax.15 = f32[128]{0:T(128)S(1)} all-reduce(f32[128]{0:T(128)S(1)} %bitcast.414), channel_id=1, replica_groups=mesh['ctx_0'=16,'ctx_1'=4,'head'=8] {'ctx_1'}, use_global_device_ids=true, to_apply=%region_6.7 | all-reduce | flops 128 | bytes 1024 | tf_op jit(solution)/shard_map/pmax | solution.py:41
  355.0 1.9 broadcast_compare_fusion
  357.0 3.2 collective-permute-start.1
  360.2 2.7 collective-permute-start
  363.0 5.2 collective-permute-done
  368.4 1.9 copy-done.5
  370.6 27.8 %all-gather.8 = f32[16,1,128]{2,1,0:T(1,128)S(1)} all-gather(f32[1,1,128]{2,1,0:T(1,128)S(1)} %bitcast.410), channel_id=4, replica_groups=mesh['ctx_0'=16,'ctx_1'=4,'head'=8] {'ctx_0'}, dimensions={0}, use_global_device_ids=true | all-gather | bytes 8704 | tf_op jit(solution)/shard_map/all_gather | solution.py:47
  398.4 7.0 all-gather.9
  405.5 15.1 %all-gather.14.cloned.1.call-done = f32[2048,128]{1,0:T(8,128)} async-done(((f32[128,128]{1,0:T(8,128)}), f32[2048,128]{1,0:T(8,128)}) %all-gather.14.cloned.1.call-update) | async-done | bytes 1048592 | tf_op jit(solution)/shard_map/all_gather | solution.py:47
  421.9 12.7 %all-gather.1 = f32[512,128]{1,0:T(8,128)S(1)} all-gather(f32[128,128]{1,0:T(8,128)S(1)} %reduce.31), channel_id=3, replica_groups=mesh['ctx_0'=16,'ctx_1'=4,'head'=8] {'ctx_1'}, dimensions={0}, use_global_device_ids=true | all-gather | bytes 327680 | tf_op jit(solution)/shard_map/all_gather | solution.py:47
  434.7 2.8 gather_fusion.1
  440.0 2.4 select_reduce_fusion
  444.7 1.4 copy-done.6
  446.1 2.4 select_select_fusion
  448.8 1.7 multiply_convert_fusion
  452.7 2.5 broadcast_in_dim.195
  455.2 6.7 scatter_fusion
  461.9 12.2 %all-to-all-start.6 = ((bf16[64,2,64,256]{3,2,1,0:T(8,128)(2,1)}), bf16[64,2,64,256]{3,2,1,0:T(8,128)(2,1)}, u32[]{:S(2)}, u32[]{:S(2)}) async-start(bf16[64,2,64,256]{3,2,1,0:T(8,128)(2,1)} %bitcast.340), calls=%async_computation.6 | async-start | bytes 8388608 | tf_op jit(solution)/shard_map/all_to_all | solution.py:290
  484.3 93.3 %all-gather.16.cloned.1.call-done = f32[2048,128]{1,0:T(8,128)} async-done(((f32[128,128]{1,0:T(8,128)}), f32[2048,128]{1,0:T(8,128)}) %all-gather.16.cloned.1.call-update) | async-done | bytes 1048592 | tf_op jit(solution)/shard_map/all_gather | solution.py:47
  578.9 14.4 %all-gather.5 = f32[512,128]{1,0:T(8,128)S(1)} all-gather(f32[128,128]{1,0:T(8,128)S(1)} %reduce.35), channel_id=7, replica_groups=mesh['ctx_0'=16,'ctx_1'=4,'head'=8] {'ctx_1'}, dimensions={0}, use_global_device_ids=true | all-gather | bytes 327680 | tf_op jit(solution)/shard_map/all_gather | solution.py:47
  595.7 3.5 collective-permute-start.3
  601.6 4.7 collective-permute-start.2
  611.7 1.5 fusion.18
  613.3 50.6 %collective-permute-done.2 = bf16[1,64,256]{2,1,0:T(8,128)(2,1)S(1)} collective-permute-done((bf16[1,64,256]{2,1,0:T(8,128)(2,1)S(1)}, bf16[1,64,256]{2,1,0:T(8,128)(2,1)S(1)}, u32[]{:S(2)}, u32[]{:S(2)}) %collective-permute-start.2) | collective-permute-done | bytes 32800 | tf_op jit(solution)/shard_map/ppermute | solution.py:55
  664.8 22.2 %all-gather.18.cloned.1.call-done = f32[32,1,64,256]{3,2,1,0:T(8,128)} async-done(((f32[2,1,64,256]{3,2,1,0:T(8,128)}), f32[32,1,64,256]{3,2,1,0:T(8,128)}) %all-gather.18.cloned.1.call-update) | async-done | bytes 2097168 | tf_op jit(solution)/shard_map/all_gather | solution.py:47
  687.0 1.7 bitcast_reduce_fusion.1
  688.7 13.5 %all-gather.7 = f32[8,64,256]{2,1,0:T(8,128)S(1)} all-gather(f32[2,64,256]{2,1,0:T(8,128)S(1)} %bitcast_reduce_fusion.1), channel_id=9, replica_groups=mesh['ctx_0'=16,'ctx_1'=4,'head'=8] {'ctx_1'}, dimensions={0}, use_global_device_ids=true | all-gather | bytes 655360 | tf_op jit(solution)/shard_map/all_gather | solution.py:47
  702.3 6.5 bitcast_convert_fusion
  708.9 17.0 %scatter_fusion.1 = f32[16,64,256]{2,1,0:T(8,128)S(1)} fusion(f32[16,64,256]{2,1,0:T(8,128)S(1)} %broadcast_in_dim.194, s32[128]{0:T(128)S(1)} %fusion.60, f32[128,64,256]{2,1,0:T(8,128)} %bitcast_convert_fusion), kind=kCustom, calls=%fused_computation.4 | custom fusion | flops 2097152 | bytes 25166336 | tf_op jit(solution)/shard_map/scatter-add | solution.py:300
  725.9 1.3 fusion.32
  (170 shorter events, 46.1 us)
Async XLA Ops:
  7.2 21.8 %copy-start = (bf16[128,1024]{1,0:T(8,128)(2,1)S(1)}, bf16[128,1024]{1,0:T(8,128)(2,1)}, u32[]{:S(2)}) copy-start(bf16[128,1024]{1,0:T(8,128)(2,1)} %param.14) | copy-start | bytes 786436
  9.5 347.4 %copy-start.11 = (s32[48]{0:T(128)}, s32[48]{0:T(128)S(1)}, u32[]{:S(2)}) copy-start(s32[48]{0:T(128)S(1)} %fusion.59) | copy-start | bytes 580
  11.0 30.5 %all-to-all-start.4 = ((s32[64,1,2]{2,1,0:T(1,128)}), s32[64,1,2]{2,1,0:T(1,128)S(1)}, u32[]{:S(2)}, u32[]{:S(2)}) async-start(s32[64,1,2]{2,1,0:T(1,128)} %bitcast.41), calls=%async_computation.4 | async-start | bytes 65536 | tf_op jit(solution)/shard_map/all_to_all | solution.py:130
  41.5 10.9 %all-to-all-start = ((bf16[128,8,128]{2,0,1:T(8,128)(2,1)}), bf16[128,8,128]{2,0,1:T(8,128)(2,1)S(1)}, u32[]{:S(2)}, u32[]{:S(2)}) async-start(bf16[128,8,128]{2,0,1:T(8,128)(2,1)} %copy_bitcast_fusion.3), calls=%async_computation | async-start | bytes 524288 | tf_op jit(solution)/shard_map/all_to_all | solution.py:77
  52.3 10.9 %all-to-all-start.1 = ((bf16[128,8,128]{2,0,1:T(8,128)(2,1)}), bf16[128,8,128]{2,0,1:T(8,128)(2,1)S(1)}, u32[]{:S(2)}, u32[]{:S(2)}) async-start(bf16[128,8,128]{2,0,1:T(8,128)(2,1)} %copy_bitcast_fusion.2), calls=%async_computation.1 | async-start | bytes 524288 | tf_op jit(solution)/shard_map/all_to_all | solution.py:78
  63.2 10.9 %all-to-all-start.2 = ((bf16[128,8,128]{2,0,1:T(8,128)(2,1)}), bf16[128,8,128]{2,0,1:T(8,128)(2,1)S(1)}, u32[]{:S(2)}, u32[]{:S(2)}) async-start(bf16[128,8,128]{2,0,1:T(8,128)(2,1)} %copy_bitcast_fusion.1), calls=%async_computation.2 | async-start | bytes 524288 | tf_op jit(solution)/shard_map/all_to_all | solution.py:79
  74.1 10.9 %all-to-all-start.3 = ((bf16[128,8,128]{2,0,1:T(8,128)(2,1)}), bf16[128,8,128]{2,0,1:T(8,128)(2,1)S(1)}, u32[]{:S(2)}, u32[]{:S(2)}) async-start(bf16[128,8,128]{2,0,1:T(8,128)(2,1)} %copy_bitcast_fusion), calls=%async_computation.3 | async-start | bytes 524288 | tf_op jit(solution)/shard_map/all_to_all | solution.py:80
  84.9 7.7 %copy-start.17 = (s32[2]{0:T(128)S(1)}, s32[2]{0:T(128)}, u32[]{:S(2)}) copy-start(s32[2]{0:T(128)} %param.19) | copy-start | bytes 28
  84.9 13.6 %copy-start.8 = (s32[16,1,3]{0,1,2:T(1,128)S(1)}, s32[16,1,3]{0,1,2:T(1,128)}, u32[]{:S(2)}) copy-start(s32[16,1,3]{0,1,2:T(1,128)} %param.18) | copy-start | bytes 580
  84.9 349.8 %all-to-all-start.5 = ((bf16[64,2,64,256]{3,2,1,0:T(8,128)(2,1)}), bf16[64,2,64,256]{3,2,1,0:T(8,128)(2,1)}, u32[]{:S(2)}, u32[]{:S(2)}) async-start(bf16[64,2,64,256]{3,2,1,0:T(8,128)(2,1)} %bitcast.351), calls=%async_computation.5 | async-start | bytes 8388608 | tf_op jit(solution)/shard_map/all_to_all | solution.py:131
  92.6 161.3 %all-reduce.5.cloned.1.call-start = ((), (), s32[]{:S(2)}) async-start(), calls=%async_computation.10 | async-start | bytes 262144 | tf_op jit(solution)/shard_map/psum | solution.py:35
  99.4 213.0 %all-reduce.7.cloned.1.call-start = ((), (), s32[]{:S(2)}) async-start(), calls=%async_computation.11 | async-start | bytes 262144 | tf_op jit(solution)/shard_map/psum | solution.py:35
  256.9 163.7 %all-gather.14.cloned.1.call-start = ((), (), s32[]{:S(2)}) async-start(), calls=%async_computation.7 | async-start | bytes 1114112 | tf_op jit(solution)/shard_map/all_gather | solution.py:47
  357.0 5.9 collective-permute-start.1
  360.2 7.9 %collective-permute-start = (bf16[64,256]{1,0:T(8,128)(2,1)S(1)}, bf16[64,256]{1,0:T(8,128)(2,1)S(1)}, u32[]{:S(2)}, u32[]{:S(2)}) collective-permute-start(bf16[64,256]{1,0:T(8,128)(2,1)S(1)} %get-tuple-element.65), channel_id=1, source_target_pairs={{0,8},{8,16},{16,24},{24,32},{32,40},{40,48},{48,56},{56,64},{64,7... | collective-permute-start | bytes 98312 | tf_op jit(solution)/shard_map/ppermute | solution.py:23
  368.4 2.0 copy-start.5
  405.4 15.2 %copy-start.15 = (f32[128]{0:T(128)}, f32[128]{0:T(128)S(1)}, u32[]{:S(2)}) copy-start(f32[128]{0:T(128)S(1)} %reduce.34) | copy-start | bytes 1540
  405.5 29.1 %copy-start.9 = (f32[2,64]{1,0:T(2,128)}, f32[2,64]{1,0:T(2,128)S(1)}, u32[]{:S(2)}) copy-start(f32[2,64]{1,0:T(2,128)S(1)} %div.95) | copy-start | bytes 1540
  443.5 2.5 copy-start.6
  443.6 2.5 copy-start.13
  443.6 2.5 copy-start.14
  444.7 7.1 copy-start.2
  450.5 2.0 copy-start.3
  452.5 2.7 copy-start.12
  461.9 12.3 %copy-start.10 = (f32[2,64]{1,0:T(2,128)S(1)}, f32[2,64]{1,0:T(2,128)}, u32[]{:S(2)}) copy-start(f32[2,64]{1,0:T(2,128)} %copy-done.9) | copy-start | bytes 1540
  461.9 12.5 %copy-start.16 = (f32[128]{0:T(128)S(1)}, f32[128]{0:T(128)}, u32[]{:S(2)}) copy-start(f32[128]{0:T(128)} %copy-done.15) | copy-start | bytes 1540
  461.9 240.3 %all-to-all-start.6 = ((bf16[64,2,64,256]{3,2,1,0:T(8,128)(2,1)}), bf16[64,2,64,256]{3,2,1,0:T(8,128)(2,1)}, u32[]{:S(2)}, u32[]{:S(2)}) async-start(bf16[64,2,64,256]{3,2,1,0:T(8,128)(2,1)} %bitcast.340), calls=%async_computation.6 | async-start | bytes 8388608 | tf_op jit(solution)/shard_map/all_to_all | solution.py:290
  474.2 103.4 %all-gather.16.cloned.1.call-start = ((), (), s32[]{:S(2)}) async-start(), calls=%async_computation.8 | async-start | bytes 1114112 | tf_op jit(solution)/shard_map/all_gather | solution.py:47
  475.6 211.4 %all-gather.18.cloned.1.call-start = ((), (), s32[]{:S(2)}) async-start(), calls=%async_computation.9 | async-start | bytes 2228224 | tf_op jit(solution)/shard_map/all_gather | solution.py:47
  595.7 69.1 %collective-permute-start.3 = (bf16[1,64,256]{2,1,0:T(8,128)(2,1)S(1)}, bf16[1,64,256]{2,1,0:T(8,128)(2,1)S(1)}, u32[]{:S(2)}, u32[]{:S(2)}) collective-permute-start(bf16[1,64,256]{2,1,0:T(8,128)(2,1)S(1)} %fusion.57), channel_id=1, source_target_pairs={{0,8},{8,16},{16,24},{24,32},{32,40},{40,48},{48,56},{56,64},{64,7... | collective-permute-start | bytes 98312 | tf_op jit(solution)/shard_map/ppermute | solution.py:55
  601.6 62.2 %collective-permute-start.2 = (bf16[1,64,256]{2,1,0:T(8,128)(2,1)S(1)}, bf16[1,64,256]{2,1,0:T(8,128)(2,1)S(1)}, u32[]{:S(2)}, u32[]{:S(2)}) collective-permute-start(bf16[1,64,256]{2,1,0:T(8,128)(2,1)S(1)} %fusion.54), channel_id=1, source_target_pairs={{8,0},{16,8},{24,16},{32,24},{40,32},{48,40},{56,48},{64,56},{72,6... | collective-permute-start | bytes 98312 | tf_op jit(solution)/shard_map/ppermute | solution.py:55
  608.8 1.6 copy-start.4
  608.8 2.8 copy-start.7
  708.9 19.3 %copy-start.1 = (bf16[128,1024]{1,0:T(8,128)(2,1)S(1)}, bf16[128,1024]{1,0:T(8,128)(2,1)}, u32[]{:S(2)}) copy-start(bf16[128,1024]{1,0:T(8,128)(2,1)} %param.14) | copy-start | bytes 786436
Sparse Core Ops, SparseCore 0:
  99.6 154.3 all-reduce.4
  257.1 55.3 all-reduce.6
  353.0 67.5 all-gather.13
  477.3 100.2 all-gather.15
  580.1 106.8 all-gather.17
